TPU v7x, 128 devices: a whole 4x4x4 slice. The times are simulated.
128 devices in a mesh: sub: 8 (over z, core), row: 4 (over x), col: 4 (over y).
Axes of the slice: x: 4, y: 4, z: 4, core: 2. Of those that a mesh axis runs over, the one named last changes fastest.
Arguments:
- front: float32 [4, 32, 128, 32, 4, 128], P(None, ('sub', 'row'), None, None, 'col'), may hold values from -2.4 to 7.5, as said below
- child_tiles: bfloat16 [16384, 128, 128], P(('sub', 'row', 'col')), may hold values from -2.390625 to 2.390625
- tile_owner: int32 [16384, 1], P(('sub', 'row', 'col')), may hold values from 0 to 127; in each aligned block of 128 rows (0 to 127, 128 to 255, ...) at most 2 rows name the same one
- tile_slot: int32 [16384], P(('sub', 'row', 'col')), may hold values from 2 to 127
Outputs:
- updated: float32 [4, 32, 128, 32, 4, 128], P(None, ('sub', 'row'), None, None, 'col')
- panel: bfloat16 [4, 32, 128, 2, 4, 128], P(None, ('sub', 'row'), None, None, 'col')
Inputs may be any that keep to these rules, and one draw needn't show every extreme that they name: The leading 1024 x 1024 block of front, made symmetric from its lower triangle, is positive definite. `tile_owner`: at most 2 of the tiles of one device go to one owner.
All inputs are finite; a program needn't handle non-finite values.
Results may differ from a plain program's by a relative error of at most 0.0038.
Values may be sent and summed in bfloat16 or wider, within the bound.
A program may use at most 128 MiB of HBM per device.

v0:
```python
import jax
import jax.numpy as jnp
from jax import lax
from jax.sharding import PartitionSpec as P

NB = 1024


def broadcast(block, axis, source):
    block = jnp.where(lax.axis_index(axis) == source, block, jnp.zeros_like(block))
    return lax.psum(block, axis)


def local(front, child_tiles, tile_owner, tile_slot):
    row_tiles, _, tile_size, col_tiles, _, _ = front.shape
    sub_count = lax.axis_size("sub")
    row_count = lax.axis_size("row")
    col_count = lax.axis_size("col")
    dev_count = sub_count * row_count * col_count
    tile_count = child_tiles.shape[0]
    capacity = max(2, 2 * tile_count // dev_count)
    panel_tiles = NB // tile_size
    per_col = panel_tiles // col_count
    height = row_tiles * tile_size
    local_front = front.reshape(row_tiles, tile_size, col_tiles, tile_size)
    owners = tile_owner[:, 0]
    matches = (owners[:, None] == jnp.arange(dev_count, dtype=jnp.int32)[None, :]).astype(jnp.int32)
    before = jnp.cumsum(matches, 0) - matches
    placed = jnp.sum(before * matches, 1)
    outgoing = (
        jnp.zeros((dev_count, capacity, tile_size, tile_size), jnp.bfloat16)
        .at[owners, placed]
        .set(child_tiles)
    )
    targets = jnp.full((dev_count, capacity), -1, jnp.int32).at[owners, placed].set(tile_slot)
    arrived, landing = (
        lax.all_to_all(outgoing, ("sub", "row", "col"), split_axis=0, concat_axis=0, tiled=True),
        lax.all_to_all(targets, ("sub", "row", "col"), split_axis=0, concat_axis=0, tiled=True),
    )
    arrived = arrived.reshape(dev_count * capacity, tile_size, tile_size)
    landing = landing.reshape(dev_count * capacity)
    selector = (
        landing[:, None] == jnp.arange(row_tiles * col_tiles, dtype=jnp.int32)[None, :]
    ).astype(jnp.bfloat16)
    selector = selector.reshape(dev_count * capacity, row_tiles, col_tiles)
    assembled = local_front + jnp.einsum(
        "kqs,kab->qasb", selector, arrived, preferred_element_type=jnp.float32
    )
    sub_index = lax.axis_index("sub")
    row_index = lax.axis_index("row")
    col_index = lax.axis_index("col")
    group_id = sub_index * row_count + row_index
    corner = assembled[0, :, :per_col, :]
    beside_all = lax.all_gather(corner, ("row", "col"), axis=0, tiled=True)
    beside_all = beside_all.reshape(row_count, col_count, tile_size, per_col, tile_size)
    beside_all = beside_all.transpose(0, 2, 3, 1, 4).reshape(row_count * tile_size, NB)
    blocks = []
    for owner_sub in range(panel_tiles // row_count):
        blocks.append(broadcast(beside_all, "sub", owner_sub))
    pivot = jnp.concatenate(blocks, 0)
    symmetric = jnp.tril(pivot) + jnp.tril(pivot, -1).T
    factor = jnp.linalg.cholesky(symmetric)
    panel_cols = assembled[:, :, :per_col, :].reshape(height, per_col, 1, tile_size)
    widened = lax.all_gather(panel_cols, "col", axis=2, tiled=True).reshape(height, NB)
    solved = jax.scipy.linalg.solve_triangular(factor, widened.T, lower=True).T.astype(jnp.bfloat16)
    leading = lax.dynamic_slice_in_dim(
        factor, jnp.minimum(group_id, panel_tiles - 1) * tile_size, tile_size, 0
    ).astype(jnp.bfloat16)
    upper = jnp.where(group_id < panel_tiles, leading, solved[:tile_size])
    panel_rows = jnp.concatenate([upper, solved[tile_size:]], 0)
    panel_out = lax.dynamic_index_in_dim(
        panel_rows.reshape(row_tiles, tile_size, per_col, col_count, tile_size),
        col_index,
        3,
        keepdims=True,
    )
    panel_out = panel_out.reshape(row_tiles, 1, tile_size, per_col, 1, tile_size)
    across = broadcast(panel_rows, "row", col_index)
    update = jnp.einsum(
        "rk,nqbk->rqnb",
        panel_rows,
        lax.all_gather(across.reshape(1, row_tiles, tile_size, NB), "sub", axis=0, tiled=True),
        preferred_element_type=jnp.float32,
    )
    update = update.reshape(row_tiles, tile_size, col_tiles, tile_size)
    row_tile = jnp.arange(row_tiles, dtype=jnp.int32) * (row_count * sub_count) + group_id
    col_tile = jnp.arange(col_tiles, dtype=jnp.int32) * col_count + col_index
    trailing_mask = (row_tile >= panel_tiles)[:, None, None, None] & (col_tile >= panel_tiles)[
        None, None, :, None
    ]
    result = jnp.where(trailing_mask, assembled - update, assembled)
    return (result.reshape(front.shape), panel_out)


def solution(mesh):
    return jax.shard_map(
        local,
        mesh=mesh,
        in_specs=(
            P(None, ("sub", "row"), None, None, "col", None),
            P(("sub", "row", "col"), None, None),
            P(("sub", "row", "col"), None),
            P(("sub", "row", "col")),
        ),
        out_specs=(
            P(None, ("sub", "row"), None, None, "col", None),
            P(None, ("sub", "row"), None, None, "col", None),
        ),
        check_vma=False,
    )
```

profile of v0, /device:TPU:1, one launch (start us, length us, event | category | flops | bytes accessed | tf_op | source)
XLA Modules:
  0.0 870.7 jit_solution(1453275617700814061)
XLA Ops:
  9.6 11.0 %scatter_fusion.1 = s32[128,2]{0,1:T(2,128)S(1)} fusion(s32[128,2]{0,1:T(2,128)S(1)} %broadcast_in_dim.35, s32[128]{0:T(128)S(1)} %fusion.70, s32[128]{0:T(128)} %param.7), kind=kCustom, calls=%fused_computation.1 | custom fusion | bytes 2560 | tf_op jit(solution)/shard_map/scatter | solution.py:35
  21.3 11.5 %all-to-all-start.1 = ((s32[128,1,2]{2,1,0:T(1,128)}), s32[128,1,2]{2,1,0:T(1,128)S(1)}, u32[]{:S(2)}, u32[]{:S(2)}) async-start(s32[128,1,2]{2,1,0:T(1,128)} %copy.65), calls=%async_computation.1 | async-start | bytes 131072 | tf_op jit(solution)/shard_map/all_to_all | solution.py:38
  38.3 20.7 %scatter_fusion = bf16[128,2,128,128]{3,2,1,0:T(8,128)(2,1)} fusion(bf16[128,2,128,128]{3,2,1,0:T(8,128)(2,1)} %broadcast_in_dim.34, s32[128]{0:T(128)S(1)} %fusion.70, bf16[128,128,128]{2,1,0:T(8,128)(2,1)} %param.5), kind=kCustom, calls=%fused_computation | custom fusion | bytes 12583936 | tf_op jit(solution)/shard_map/scatter | solution.py:33
  59.1 10.2 %all-to-all-start = ((bf16[128,2,128,128]{3,2,1,0:T(8,128)(2,1)}), bf16[128,2,128,128]{3,2,1,0:T(8,128)(2,1)}, u32[]{:S(2)}, u32[]{:S(2)}) async-start(bf16[128,2,128,128]{3,2,1,0:T(8,128)(2,1)} %scatter_fusion), calls=%async_computation | async-start | bytes 16777216 | tf_op jit(solution)/shard_map/all_to_all | solution.py:37
  70.8 99.1 %all-to-all-done = bf16[128,2,128,128]{3,2,1,0:T(8,128)(2,1)} async-done(((bf16[128,2,128,128]{3,2,1,0:T(8,128)(2,1)}), bf16[128,2,128,128]{3,2,1,0:T(8,128)(2,1)}, u32[]{:S(2)}, u32[]{:S(2)}) %all-to-all-start) | async-done | bytes 8388640 | tf_op jit(solution)/shard_map/all_to_all | solution.py:37
  169.9 12.2 %copy.64 = bf16[128,2,128,128]{3,1,0,2:T(2,128)(2,1)S(1)} copy(bf16[128,2,128,128]{3,2,1,0:T(8,128)(2,1)} %all-to-all-done) | data formatting | bytes 16777216 | tf_op jit(solution)/shard_map/all_to_all | solution.py:37
  194.4 40.8 %all-gather.9.cloned.1.call-done = f32[1,2048,2,128]{3,2,0,1:T(2,128)} async-done(((f32[1,128,2,128]{3,2,0,1:T(2,128)}), f32[1,2048,2,128]{3,2,0,1:T(2,128)}) %all-gather.9.cloned.1.call-update) | async-done | bytes 2097168 | tf_op jit(solution)/shard_map/all_gather | solution.py:54
  249.6 18.8 %all-gather.5.cloned.1.call-done = f32[512,2,4,128]{3,0,1,2:T(8,128)} async-done(((f32[512,2,1,128]{3,0,1,2:T(8,128)}), f32[512,2,4,128]{3,0,1,2:T(8,128)}) %all-gather.5.cloned.1.call-update) | async-done | bytes 2097168 | tf_op jit(solution)/shard_map/all_gather | solution.py:64
  270.4 71.8 %all-reduce.7.cloned.1.call-done = (f32[512,1024]{1,0:T(8,128)}, f32[512,1024]{1,0:T(8,128)}) async-done(((f32[512,1024]{1,0:T(8,128)}, f32[512,1024]{1,0:T(8,128)}), (f32[512,1024]{1,0:T(8,128)}, f32[512,1024]{1,0:T(8,128)})) %all-reduce.7.cloned.1.call-update) | async-done | bytes 4194320 | tf_op jit(solution)/shard_map/psum | solution.py:11
  372.2 11.7 %cholesky.222 = f32[128,128]{1,0:T(8,128)S(1)} custom-call(f32[128,128]{1,0:T(8,128)S(1)} %cholesky.577), custom_call_target="Cholesky" | custom-call | tf_op jit(solution)/shard_map/jit(cholesky)/cholesky | solution.py:62
  386.5 9.8 %custom-call.63 = f32[1,128,128]{1,2,0:T(8,128)S(1)} custom-call(f32[1,128,128]{2,1,0:T(8,128)S(1)} %get-tuple-element.74), custom_call_target="InvertDiagBlocksLowerTriangular" | custom-call | tf_op jit(solution)/shard_map/jit(cholesky)/cholesky | solution.py:62
  400.2 12.1 %cholesky.243 = f32[128,128]{1,0:T(8,128)S(1)} custom-call(f32[128,128]{1,0:T(8,128)S(1)} %cholesky.581), custom_call_target="Cholesky" | custom-call | tf_op jit(solution)/shard_map/jit(cholesky)/cholesky | solution.py:62
  413.0 9.8 %custom-call.64 = f32[1,128,128]{1,2,0:T(8,128)S(1)} custom-call(f32[1,128,128]{2,1,0:T(8,128)S(1)} %get-tuple-element.71), custom_call_target="InvertDiagBlocksLowerTriangular" | custom-call | tf_op jit(solution)/shard_map/jit(cholesky)/cholesky | solution.py:62
  426.1 11.7 %cholesky.466 = f32[128,128]{1,0:T(8,128)S(1)} custom-call(f32[128,128]{1,0:T(8,128)S(1)} %cholesky.586), custom_call_target="Cholesky" | custom-call | tf_op jit(solution)/shard_map/jit(cholesky)/cholesky | solution.py:62
  439.1 9.8 %custom-call.65 = f32[1,128,128]{1,2,0:T(8,128)S(1)} custom-call(f32[1,128,128]{2,1,0:T(8,128)S(1)} %get-tuple-element.68), custom_call_target="InvertDiagBlocksLowerTriangular" | custom-call | tf_op jit(solution)/shard_map/jit(cholesky)/cholesky | solution.py:62
  452.4 11.8 %cholesky.485 = f32[128,128]{1,0:T(8,128)S(1)} custom-call(f32[128,128]{1,0:T(8,128)S(1)} %cholesky.591), custom_call_target="Cholesky" | custom-call | tf_op jit(solution)/shard_map/jit(cholesky)/cholesky | solution.py:62
  465.6 9.8 %custom-call.66 = f32[1,128,128]{1,2,0:T(8,128)S(1)} custom-call(f32[1,128,128]{2,1,0:T(8,128)S(1)} %get-tuple-element.65), custom_call_target="InvertDiagBlocksLowerTriangular" | custom-call | tf_op jit(solution)/shard_map/jit(cholesky)/cholesky | solution.py:62
  478.8 11.7 %cholesky.504 = f32[128,128]{1,0:T(8,128)S(1)} custom-call(f32[128,128]{1,0:T(8,128)S(1)} %cholesky.596), custom_call_target="Cholesky" | custom-call | tf_op jit(solution)/shard_map/jit(cholesky)/cholesky | solution.py:62
  491.8 10.0 %custom-call.67 = f32[1,128,128]{1,2,0:T(8,128)S(1)} custom-call(f32[1,128,128]{2,1,0:T(8,128)S(1)} %get-tuple-element.62), custom_call_target="InvertDiagBlocksLowerTriangular" | custom-call | tf_op jit(solution)/shard_map/jit(cholesky)/cholesky | solution.py:62
  505.2 11.7 %cholesky.524 = f32[128,128]{1,0:T(8,128)S(1)} custom-call(f32[128,128]{1,0:T(8,128)S(1)} %cholesky.601), custom_call_target="Cholesky" | custom-call | tf_op jit(solution)/shard_map/jit(cholesky)/cholesky | solution.py:62
  518.1 9.8 %custom-call.68 = f32[1,128,128]{1,2,0:T(8,128)S(1)} custom-call(f32[1,128,128]{2,1,0:T(8,128)S(1)} %get-tuple-element.59), custom_call_target="InvertDiagBlocksLowerTriangular" | custom-call | tf_op jit(solution)/shard_map/jit(cholesky)/cholesky | solution.py:62
  531.0 12.1 %cholesky.544 = f32[128,128]{1,0:T(8,128)S(1)} custom-call(f32[128,128]{1,0:T(8,128)S(1)} %cholesky.606), custom_call_target="Cholesky" | custom-call | tf_op jit(solution)/shard_map/jit(cholesky)/cholesky | solution.py:62
  544.3 9.8 %custom-call.69 = f32[1,128,128]{1,2,0:T(8,128)S(1)} custom-call(f32[1,128,128]{2,1,0:T(8,128)S(1)} %get-tuple-element.56), custom_call_target="InvertDiagBlocksLowerTriangular" | custom-call | tf_op jit(solution)/shard_map/jit(cholesky)/cholesky | solution.py:62
  556.7 11.7 %cholesky.562 = f32[128,128]{1,0:T(8,128)S(1)} custom-call(f32[128,128]{1,0:T(8,128)S(1)} %convolution_subtract_fusion.13), custom_call_target="Cholesky" | custom-call | tf_op jit(solution)/shard_map/jit(cholesky)/cholesky | solution.py:62
  581.1 27.9 %while.1 = (s32[]{:T(128)}, f32[1024,1024]{1,0:T(8,128)}, s32[8,2]{0,1:T(2,128)S(1)}, f32[8,128,128]{2,1,0:T(8,128)}, s32[]{:T(128)}) while((s32[]{:T(128)}, f32[1024,1024]{1,0:T(8,128)}, s32[8,2]{0,1:T(2,128)S(1)}, f32[8,128,128]{2,1,0:T(8,128)}, s32[]{:T(128)}) %tuple.68), condition=%wide.while_cond, body=%wide.while_body.sunk | while | flops 2 | bytes 132705 | solution.py:65
  609.0 79.6 %custom-call.70 = f32[8,128,128]{1,2,0:T(8,128)S(1)} custom-call(f32[8,128,128]{2,1,0:T(8,128)} %get-tuple-element.9), custom_call_target="InvertDiagBlocksLowerTriangular" | custom-call | tf_op jit(solution)/shard_map/jit(_solve_triangular)/triangular_solve | solution.py:65
  719.9 45.9 %all-reduce.5.cloned.1.call-done = bf16[1,4,128,1024]{3,2,1,0:T(8,128)(2,1)} async-done(((bf16[1,4,128,1024]{3,2,1,0:T(8,128)(2,1)}), bf16[1,4,128,1024]{3,2,1,0:T(8,128)(2,1)}) %all-reduce.5.cloned.1.call-update) | async-done | bytes 1048592 | tf_op jit(solution)/shard_map/psum | solution.py:11
  768.5 52.0 %all-gather.7.cloned.1.call-done = bf16[8,4,128,1024]{3,2,1,0:T(8,128)(2,1)} async-done(((bf16[1,4,128,1024]{3,2,1,0:T(8,128)(2,1)}), bf16[8,4,128,1024]{3,2,1,0:T(8,128)(2,1)}) %all-gather.7.cloned.1.call-update) | async-done | bytes 8388624 | tf_op jit(solution)/shard_map/all_gather | solution.py:82
  820.5 10.4 %convolution_bitcast_fusion = f32[512,4,8,128]{0,3,1,2:T(8,128)} fusion(bf16[8,4,128,1024]{3,2,1,0:T(8,128)(2,1)} %all-gather.7.cloned.1.call-done, bf16[384,1024]{1,0:T(8,128)(2,1)S(1)} %slice.280, bf16[128,1024]{1,0:T(8,128)(2,1)S(1)} %fusion.36), kind=kOutput, calls=%fused_computation.15 | convolution fusion | flops 4297064448 | bytes 17825792 | tf_op jit(solution)/shard_map/rk,nqbk->rqnb/dot_general | solution.py:79
  830.8 10.4 %copy.80 = f32[512,4,8,128]{3,2,1,0:T(8,128)} copy(f32[512,4,8,128]{0,3,1,2:T(8,128)} %convolution_bitcast_fusion) | data formatting | bytes 16777216 | tf_op jit(solution)/shard_map/rk,nqbk->rqnb/transpose | solution.py:79
  841.3 11.7 %fusion = f32[4,1,128,32,1,128]{5,3,0,2,4,1:T(8,128)} fusion(f32[4,128,32,128]{3,2,0,1:T(8,128)} %copy-done, f32[4,128,32,128]{3,2,1,0:T(8,128)} %bitcast.154, pred[4,32]{1,0:T(4,128)(4,1)S(1)} %broadcast_and_fusion), kind=kLoop, calls=%fused_computation.5 | loop fusion | flops 4194304 | bytes 25165952 | tf_op jit(solution)/shard_map/reshape | solution.py:92
  853.0 11.0 %copy.83 = f32[4,1,128,32,1,128]{5,4,3,2,1,0:T(1,128)} copy(f32[4,1,128,32,1,128]{5,3,0,2,4,1:T(8,128)} %fusion) | data formatting | bytes 16777216
  (154 shorter events, 170.7 us)
Async XLA Ops:
  21.3 37.7 %all-to-all-start.1 = ((s32[128,1,2]{2,1,0:T(1,128)}), s32[128,1,2]{2,1,0:T(1,128)S(1)}, u32[]{:S(2)}, u32[]{:S(2)}) async-start(s32[128,1,2]{2,1,0:T(1,128)} %copy.65), calls=%async_computation.1 | async-start | bytes 131072 | tf_op jit(solution)/shard_map/all_to_all | solution.py:38
  59.1 110.8 %all-to-all-start = ((bf16[128,2,128,128]{3,2,1,0:T(8,128)(2,1)}), bf16[128,2,128,128]{3,2,1,0:T(8,128)(2,1)}, u32[]{:S(2)}, u32[]{:S(2)}) async-start(bf16[128,2,128,128]{3,2,1,0:T(8,128)(2,1)} %scatter_fusion), calls=%async_computation | async-start | bytes 16777216 | tf_op jit(solution)/shard_map/all_to_all | solution.py:37
  69.3 165.9 %all-gather.9.cloned.1.call-start = ((), (), s32[]{:S(2)}) async-start(), calls=%async_computation.5 | async-start | bytes 2228224 | tf_op jit(solution)/shard_map/all_gather | solution.py:54
  187.2 3.4 copy-start
  191.4 77.1 %all-gather.5.cloned.1.call-start = ((), (), s32[]{:S(2)}) async-start(), calls=%async_computation.2 | async-start | bytes 2621440 | tf_op jit(solution)/shard_map/all_gather | solution.py:64
  194.2 148.1 %all-reduce.7.cloned.1.call-start = ((), (), s32[]{:S(2)}) async-start(), calls=%async_computation.6 | async-start | bytes 8388608 | tf_op jit(solution)/shard_map/psum | solution.py:11
  249.5 516.3 %all-reduce.5.cloned.1.call-start = ((), (), s32[]{:S(2)}) async-start(), calls=%async_computation.3 | async-start | bytes 2097152 | tf_op jit(solution)/shard_map/psum | solution.py:11
  342.2 2.2 copy-start.3
  344.7 1.9 copy-start.1
  370.3 1.9 copy-start.2
  688.6 8.2 copy-start.4
  719.9 100.6 %all-gather.7.cloned.1.call-start = ((), (), s32[]{:S(2)}) async-start(), calls=%async_computation.4 | async-start | bytes 9437184 | tf_op jit(solution)/shard_map/all_gather | solution.py:82
Sparse Core Ops, SparseCore 0:
  191.5 43.6 all-gather.8
  236.9 31.5 all-gather.4
  270.9 71.2 all-reduce.6
  720.0 45.8 all-reduce.4
  767.4 53.0 all-gather.6
where the time goes:
time: 878 us; the launch traced here: 871 us
  waiting for transfers between devices  329 us (37%)
  other arithmetic  291 us (33%)
  local copies, waits for them, and re-layouts  144 us (16%)
  matrix products  66.1 us (8%)
  starting transfers between devices  22.1 us (3%)
  between operations  19.5 us (2%)
    another operation x30, other arithmetic, local(): factor = jnp.linalg.cholesky(symmetric)  172 us
    psum x2, waiting for transfers between devices, broadcast(): return lax.psum(block, axis)  118 us
    all_to_all x1, waiting for transfers between devices, local(): lax.all_to_all(outgoing, ('sub', 'row', 'col'), split_axis=0, concat_axis...  99.1 us
    another operation x3, other arithmetic, local(): jax.scipy.linalg.solve_triangular(factor, widened.T, lower=True)  85.4 us
    all_gather x1, waiting for transfers between devices, local(): lax.all_gather(across.reshape(1, row_tiles, tile_size, NB), 'sub', axis=0...  52 us
    all_gather x1, waiting for transfers between devices, local(): beside_all = lax.all_gather(corner, ('row', 'col'), axis=0, tiled=True)  40.8 us
    another operation x24, local copies, waits for them, and re-layouts  27.9 us
    another operation x15, matrix products, local(): jax.scipy.linalg.solve_triangular(factor, widened.T, lower=True)  27.5 us
  transfers between devices with their start and end apart: 7, of which 6 were waited for; matrix products, arithmetic and copies ran while one was open for 6% of the time, Pallas kernels for 0%

commit v1 on v0

--- a/solution.py
+++ b/solution.py
@@ -4,6 +4,13 @@
 from jax.sharding import PartitionSpec as P
 
 NB = 1024
+
+
+def exchange_gather(x, mesh_axis, dim):
+    peers = lax.axis_size(mesh_axis)
+    blocks = jnp.stack([x for _ in range(peers)])
+    blocks = lax.all_to_all(blocks, mesh_axis, split_axis=0, concat_axis=0)
+    return jnp.concatenate(blocks, axis=dim)
 
 
 def broadcast(block, axis, source):
@@ -79,7 +86,7 @@
     update = jnp.einsum(
         "rk,nqbk->rqnb",
         panel_rows,
-        lax.all_gather(across.reshape(1, row_tiles, tile_size, NB), "sub", axis=0, tiled=True),
+        exchange_gather(across.reshape(1, row_tiles, tile_size, NB), "sub", 0),
         preferred_element_type=jnp.float32,
     )
     update = update.reshape(row_tiles, tile_size, col_tiles, tile_size)

time: 878 us -> 931 us (1.060)
  waiting for transfers between devices: 329 us -> 368 us
    all_to_all x0 -> x1, waiting for transfers between devices: none -> 91.2 us  [exchange_gather(): blocks = lax.all_to_all(blocks, mesh_axis, split_axis=0, concat_axis=0)]
    all_gather x1 -> x0, waiting for transfers between devices: 52 us -> none  [local(): lax.all_gather(across.reshape(1, row_tiles, tile_size, NB), 'sub', axis=0...]
    another operation x24 -> x25, local copies, waits for them, and re-layouts: 27.9 us -> 33.4 us
  transfers between devices with their start and end apart: 7 -> 7, of which waited for: 6 -> 6; matrix products, arithmetic and copies ran while one was open for 6% -> 5% of each run, Pallas kernels for 0% -> 0%
where the time goes in v1:
time: 931 us; the launch traced here: 923 us
  waiting for transfers between devices  368 us (40%)
  other arithmetic  291 us (31%)
  local copies, waits for them, and re-layouts  149 us (16%)
  matrix products  66.1 us (7%)
  starting transfers between devices  29.6 us (3%)
  between operations  19.4 us (2%)
    another operation x30, other arithmetic, local(): factor = jnp.linalg.cholesky(symmetric)  172 us
    psum x2, waiting for transfers between devices, broadcast(): return lax.psum(block, axis)  118 us
    all_to_all x1, waiting for transfers between devices, local(): lax.all_to_all(outgoing, ('sub', 'row', 'col'), split_axis=0, concat_axis...  99.1 us
    all_to_all x1, waiting for transfers between devices, exchange_gather(): blocks = lax.all_to_all(blocks, mesh_axis, split_axis=0, concat_axis=0)  91.2 us
    another operation x3, other arithmetic, local(): jax.scipy.linalg.solve_triangular(factor, widened.T, lower=True)  85.4 us
    all_gather x1, waiting for transfers between devices, local(): beside_all = lax.all_gather(corner, ('row', 'col'), axis=0, tiled=True)  40.8 us
    another operation x24, local copies, waits for them, and re-layouts  27.9 us
    another operation x15, matrix products, local(): jax.scipy.linalg.solve_triangular(factor, widened.T, lower=True)  27.5 us
  transfers between devices with their start and end apart: 7, of which 6 were waited for; matrix products, arithmetic and copies ran while one was open for 5% of the time, Pallas kernels for 0%

profile of v1, /device:TPU:1, one launch (start us, length us, event | category | flops | bytes accessed | tf_op | source)
XLA Modules:
  0.0 922.9 jit_solution(8403412075255145358)
XLA Ops:
  9.6 11.0 %scatter_fusion.1 = s32[128,2]{0,1:T(2,128)S(1)} fusion(s32[128,2]{0,1:T(2,128)S(1)} %broadcast_in_dim.35, s32[128]{0:T(128)S(1)} %fusion.75, s32[128]{0:T(128)} %param.7), kind=kCustom, calls=%fused_computation.1 | custom fusion | bytes 2560 | tf_op jit(solution)/shard_map/scatter | solution.py:42
  21.3 11.5 %all-to-all-start.1 = ((s32[128,1,2]{2,1,0:T(1,128)}), s32[128,1,2]{2,1,0:T(1,128)S(1)}, u32[]{:S(2)}, u32[]{:S(2)}) async-start(s32[128,1,2]{2,1,0:T(1,128)} %copy.65), calls=%async_computation.1 | async-start | bytes 131072 | tf_op jit(solution)/shard_map/all_to_all | solution.py:45
  38.3 20.7 %scatter_fusion = bf16[128,2,128,128]{3,2,1,0:T(8,128)(2,1)} fusion(bf16[128,2,128,128]{3,2,1,0:T(8,128)(2,1)} %broadcast_in_dim.34, s32[128]{0:T(128)S(1)} %fusion.75, bf16[128,128,128]{2,1,0:T(8,128)(2,1)} %param.5), kind=kCustom, calls=%fused_computation | custom fusion | bytes 12583936 | tf_op jit(solution)/shard_map/scatter | solution.py:40
  59.1 10.2 %all-to-all-start = ((bf16[128,2,128,128]{3,2,1,0:T(8,128)(2,1)}), bf16[128,2,128,128]{3,2,1,0:T(8,128)(2,1)}, u32[]{:S(2)}, u32[]{:S(2)}) async-start(bf16[128,2,128,128]{3,2,1,0:T(8,128)(2,1)} %scatter_fusion), calls=%async_computation | async-start | bytes 16777216 | tf_op jit(solution)/shard_map/all_to_all | solution.py:44
  70.8 99.1 %all-to-all-done = bf16[128,2,128,128]{3,2,1,0:T(8,128)(2,1)} async-done(((bf16[128,2,128,128]{3,2,1,0:T(8,128)(2,1)}), bf16[128,2,128,128]{3,2,1,0:T(8,128)(2,1)}, u32[]{:S(2)}, u32[]{:S(2)}) %all-to-all-start) | async-done | bytes 8388640 | tf_op jit(solution)/shard_map/all_to_all | solution.py:44
  169.9 12.2 %copy.64 = bf16[128,2,128,128]{3,1,0,2:T(2,128)(2,1)S(1)} copy(bf16[128,2,128,128]{3,2,1,0:T(8,128)(2,1)} %all-to-all-done) | data formatting | bytes 16777216 | tf_op jit(solution)/shard_map/all_to_all | solution.py:44
  194.4 40.8 %all-gather.6.cloned.1.call-done = f32[1,2048,2,128]{3,2,0,1:T(2,128)} async-done(((f32[1,128,2,128]{3,2,0,1:T(2,128)}), f32[1,2048,2,128]{3,2,0,1:T(2,128)}) %all-gather.6.cloned.1.call-update) | async-done | bytes 2097168 | tf_op jit(solution)/shard_map/all_gather | solution.py:61
  249.6 18.8 %all-gather.4.cloned.1.call-done = f32[512,2,4,128]{3,0,1,2:T(8,128)} async-done(((f32[512,2,1,128]{3,0,1,2:T(8,128)}), f32[512,2,4,128]{3,0,1,2:T(8,128)}) %all-gather.4.cloned.1.call-update) | async-done | bytes 2097168 | tf_op jit(solution)/shard_map/all_gather | solution.py:71
  270.4 71.8 %all-reduce.7.cloned.1.call-done = (f32[512,1024]{1,0:T(8,128)}, f32[512,1024]{1,0:T(8,128)}) async-done(((f32[512,1024]{1,0:T(8,128)}, f32[512,1024]{1,0:T(8,128)}), (f32[512,1024]{1,0:T(8,128)}, f32[512,1024]{1,0:T(8,128)})) %all-reduce.7.cloned.1.call-update) | async-done | bytes 4194320 | tf_op jit(solution)/shard_map/psum | solution.py:18
  372.2 11.7 %cholesky.222 = f32[128,128]{1,0:T(8,128)S(1)} custom-call(f32[128,128]{1,0:T(8,128)S(1)} %cholesky.577), custom_call_target="Cholesky" | custom-call | tf_op jit(solution)/shard_map/jit(cholesky)/cholesky | solution.py:69
  386.5 9.8 %custom-call.63 = f32[1,128,128]{1,2,0:T(8,128)S(1)} custom-call(f32[1,128,128]{2,1,0:T(8,128)S(1)} %get-tuple-element.74), custom_call_target="InvertDiagBlocksLowerTriangular" | custom-call | tf_op jit(solution)/shard_map/jit(cholesky)/cholesky | solution.py:69
  400.2 12.1 %cholesky.243 = f32[128,128]{1,0:T(8,128)S(1)} custom-call(f32[128,128]{1,0:T(8,128)S(1)} %cholesky.581), custom_call_target="Cholesky" | custom-call | tf_op jit(solution)/shard_map/jit(cholesky)/cholesky | solution.py:69
  413.0 9.8 %custom-call.64 = f32[1,128,128]{1,2,0:T(8,128)S(1)} custom-call(f32[1,128,128]{2,1,0:T(8,128)S(1)} %get-tuple-element.71), custom_call_target="InvertDiagBlocksLowerTriangular" | custom-call | tf_op jit(solution)/shard_map/jit(cholesky)/cholesky | solution.py:69
  426.1 11.7 %cholesky.466 = f32[128,128]{1,0:T(8,128)S(1)} custom-call(f32[128,128]{1,0:T(8,128)S(1)} %cholesky.586), custom_call_target="Cholesky" | custom-call | tf_op jit(solution)/shard_map/jit(cholesky)/cholesky | solution.py:69
  439.1 9.8 %custom-call.65 = f32[1,128,128]{1,2,0:T(8,128)S(1)} custom-call(f32[1,128,128]{2,1,0:T(8,128)S(1)} %get-tuple-element.68), custom_call_target="InvertDiagBlocksLowerTriangular" | custom-call | tf_op jit(solution)/shard_map/jit(cholesky)/cholesky | solution.py:69
  452.4 11.8 %cholesky.485 = f32[128,128]{1,0:T(8,128)S(1)} custom-call(f32[128,128]{1,0:T(8,128)S(1)} %cholesky.591), custom_call_target="Cholesky" | custom-call | tf_op jit(solution)/shard_map/jit(cholesky)/cholesky | solution.py:69
  465.6 9.8 %custom-call.66 = f32[1,128,128]{1,2,0:T(8,128)S(1)} custom-call(f32[1,128,128]{2,1,0:T(8,128)S(1)} %get-tuple-element.65), custom_call_target="InvertDiagBlocksLowerTriangular" | custom-call | tf_op jit(solution)/shard_map/jit(cholesky)/cholesky | solution.py:69
  478.8 11.7 %cholesky.504 = f32[128,128]{1,0:T(8,128)S(1)} custom-call(f32[128,128]{1,0:T(8,128)S(1)} %cholesky.596), custom_call_target="Cholesky" | custom-call | tf_op jit(solution)/shard_map/jit(cholesky)/cholesky | solution.py:69
  491.8 10.0 %custom-call.67 = f32[1,128,128]{1,2,0:T(8,128)S(1)} custom-call(f32[1,128,128]{2,1,0:T(8,128)S(1)} %get-tuple-element.62), custom_call_target="InvertDiagBlocksLowerTriangular" | custom-call | tf_op jit(solution)/shard_map/jit(cholesky)/cholesky | solution.py:69
  505.2 11.7 %cholesky.524 = f32[128,128]{1,0:T(8,128)S(1)} custom-call(f32[128,128]{1,0:T(8,128)S(1)} %cholesky.601), custom_call_target="Cholesky" | custom-call | tf_op jit(solution)/shard_map/jit(cholesky)/cholesky | solution.py:69
  518.1 9.8 %custom-call.68 = f32[1,128,128]{1,2,0:T(8,128)S(1)} custom-call(f32[1,128,128]{2,1,0:T(8,128)S(1)} %get-tuple-element.59), custom_call_target="InvertDiagBlocksLowerTriangular" | custom-call | tf_op jit(solution)/shard_map/jit(cholesky)/cholesky | solution.py:69
  531.0 12.1 %cholesky.544 = f32[128,128]{1,0:T(8,128)S(1)} custom-call(f32[128,128]{1,0:T(8,128)S(1)} %cholesky.606), custom_call_target="Cholesky" | custom-call | tf_op jit(solution)/shard_map/jit(cholesky)/cholesky | solution.py:69
  544.3 9.8 %custom-call.69 = f32[1,128,128]{1,2,0:T(8,128)S(1)} custom-call(f32[1,128,128]{2,1,0:T(8,128)S(1)} %get-tuple-element.56), custom_call_target="InvertDiagBlocksLowerTriangular" | custom-call | tf_op jit(solution)/shard_map/jit(cholesky)/cholesky | solution.py:69
  556.7 11.7 %cholesky.562 = f32[128,128]{1,0:T(8,128)S(1)} custom-call(f32[128,128]{1,0:T(8,128)S(1)} %convolution_subtract_fusion.13), custom_call_target="Cholesky" | custom-call | tf_op jit(solution)/shard_map/jit(cholesky)/cholesky | solution.py:69
  581.1 27.9 %while.1 = (s32[]{:T(128)}, f32[1024,1024]{1,0:T(8,128)}, s32[8,2]{0,1:T(2,128)S(1)}, f32[8,128,128]{2,1,0:T(8,128)}, s32[]{:T(128)}) while((s32[]{:T(128)}, f32[1024,1024]{1,0:T(8,128)}, s32[8,2]{0,1:T(2,128)S(1)}, f32[8,128,128]{2,1,0:T(8,128)}, s32[]{:T(128)}) %tuple.68), condition=%wide.while_cond, body=%wide.while_body.sunk | while | flops 2 | bytes 132705 | solution.py:72
  609.0 79.6 %custom-call.70 = f32[8,128,128]{1,2,0:T(8,128)S(1)} custom-call(f32[8,128,128]{2,1,0:T(8,128)} %get-tuple-element.9), custom_call_target="InvertDiagBlocksLowerTriangular" | custom-call | tf_op jit(solution)/shard_map/jit(_solve_triangular)/triangular_solve | solution.py:72
  719.9 46.0 %all-reduce.5.cloned.1.call-done = bf16[4,128,1024]{2,1,0:T(8,128)(2,1)} async-done(((bf16[4,128,1024]{2,1,0:T(8,128)(2,1)}), bf16[4,128,1024]{2,1,0:T(8,128)(2,1)}) %all-reduce.5.cloned.1.call-update) | async-done | bytes 1048592 | tf_op jit(solution)/shard_map/psum | solution.py:18
  781.4 91.2 %all-to-all-done.2 = bf16[8,1,4,128,1024]{4,3,2,1,0:T(8,128)(2,1)} async-done(((bf16[8,1,4,128,1024]{4,3,2,1,0:T(8,128)(2,1)}), bf16[8,1,4,128,1024]{4,3,2,1,0:T(8,128)(2,1)}, u32[]{:S(2)}, u32[]{:S(2)}) %all-to-all-start.2) | async-done | bytes 8388640 | tf_op jit(solution)/shard_map/all_to_all | solution.py:12
  872.7 10.4 %fusion.6 = f32[512,4,8,128]{0,3,1,2:T(8,128)} fusion(bf16[8,1,4,128,1024]{4,3,2,1,0:T(8,128)(2,1)} %all-to-all-done.2, bf16[384,1024]{1,0:T(8,128)(2,1)S(1)} %slice.280, bf16[128,1024]{1,0:T(8,128)(2,1)S(1)} %fusion.41), kind=kOutput, calls=%fused_computation.17 | convolution fusion | flops 4297064448 | bytes 17825792 | tf_op jit(solution)/shard_map/rk,nqbk->rqnb/dot_general | solution.py:86
  883.0 10.4 %copy.80 = f32[512,4,8,128]{3,2,1,0:T(8,128)} copy(f32[512,4,8,128]{0,3,1,2:T(8,128)} %fusion.6) | data formatting | bytes 16777216 | tf_op jit(solution)/shard_map/rk,nqbk->rqnb/transpose | solution.py:86
  893.5 11.7 %fusion = f32[4,1,128,32,1,128]{5,3,0,2,4,1:T(8,128)} fusion(f32[4,128,32,128]{3,2,0,1:T(8,128)} %copy-done, f32[4,128,32,128]{3,2,1,0:T(8,128)} %bitcast.158, pred[4,32]{1,0:T(4,128)(4,1)S(1)} %broadcast_and_fusion), kind=kLoop, calls=%fused_computation.5 | loop fusion | flops 4194304 | bytes 25165952 | tf_op jit(solution)/shard_map/reshape | solution.py:99
  905.2 11.0 %copy.83 = f32[4,1,128,32,1,128]{5,4,3,2,1,0:T(1,128)} copy(f32[4,1,128,32,1,128]{5,3,0,2,4,1:T(8,128)} %fusion) | data formatting | bytes 16777216
  (154 shorter events, 183.6 us)
Async XLA Ops:
  21.3 37.7 %all-to-all-start.1 = ((s32[128,1,2]{2,1,0:T(1,128)}), s32[128,1,2]{2,1,0:T(1,128)S(1)}, u32[]{:S(2)}, u32[]{:S(2)}) async-start(s32[128,1,2]{2,1,0:T(1,128)} %copy.65), calls=%async_computation.1 | async-start | bytes 131072 | tf_op jit(solution)/shard_map/all_to_all | solution.py:45
  59.1 110.8 %all-to-all-start = ((bf16[128,2,128,128]{3,2,1,0:T(8,128)(2,1)}), bf16[128,2,128,128]{3,2,1,0:T(8,128)(2,1)}, u32[]{:S(2)}, u32[]{:S(2)}) async-start(bf16[128,2,128,128]{3,2,1,0:T(8,128)(2,1)} %scatter_fusion), calls=%async_computation | async-start | bytes 16777216 | tf_op jit(solution)/shard_map/all_to_all | solution.py:44
  69.3 165.9 %all-gather.6.cloned.1.call-start = ((), (), s32[]{:S(2)}) async-start(), calls=%async_computation.5 | async-start | bytes 2228224 | tf_op jit(solution)/shard_map/all_gather | solution.py:61
  187.2 3.4 copy-start
  191.4 77.1 %all-gather.4.cloned.1.call-start = ((), (), s32[]{:S(2)}) async-start(), calls=%async_computation.3 | async-start | bytes 2621440 | tf_op jit(solution)/shard_map/all_gather | solution.py:71
  194.2 148.1 %all-reduce.7.cloned.1.call-start = ((), (), s32[]{:S(2)}) async-start(), calls=%async_computation.6 | async-start | bytes 8388608 | tf_op jit(solution)/shard_map/psum | solution.py:18
  249.5 516.3 %all-reduce.5.cloned.1.call-start = ((), (), s32[]{:S(2)}) async-start(), calls=%async_computation.4 | async-start | bytes 2097152 | tf_op jit(solution)/shard_map/psum | solution.py:18
  342.2 2.2 copy-start.3
  344.7 1.9 copy-start.1
  370.3 1.9 copy-start.2
  688.6 8.2 copy-start.4
  771.4 101.3 %all-to-all-start.2 = ((bf16[8,1,4,128,1024]{4,3,2,1,0:T(8,128)(2,1)}), bf16[8,1,4,128,1024]{4,3,2,1,0:T(8,128)(2,1)}, u32[]{:S(2)}, u32[]{:S(2)}) async-start(bf16[8,1,4,128,1024]{4,3,2,1,0:T(8,128)(2,1)} %stack.3), calls=%async_computation.2 | async-start | bytes 16777216 | tf_op jit(solution)/shard_map/all_to_all | solution.py:12
Sparse Core Ops, SparseCore 0:
  191.5 43.6 all-gather.5
  236.9 31.5 all-gather.3
  270.9 71.2 all-reduce.6
  720.0 45.8 all-reduce.4
